TPU v7x, 256 devices: a whole 4x4x8 slice. The times are simulated.
256 devices in a mesh: slab: 64 (over y, x_lo, z), grp: 4 (over x_hi, core).
Axes of the slice: x: 4 (x_hi: 2, x_lo: 2; x = x_hi * 2 + x_lo), y: 4, z: 8, core: 2. Of those that a mesh axis runs over, the one named last changes fastest.
Arguments:
- tiles: bfloat16 [768, 27, 36864], P(('slab', 'grp')), may hold values from -0.0390625 to 0.0390625
- neighbours: int32 [768, 27], P('slab'), may hold values from 0 to 767, as said below
- t_cur: bfloat16 [768, 192, 512], P('slab', None, 'grp'), may hold values from -6 to 6
- t_prev: float32 [768, 192, 512], P('slab', None, 'grp'), may hold values from -6 to 6
- probes: float32 [768, 192, 512], P('slab', None, 'grp'), may hold values from -18 to 18
Outputs:
- t_next: float32 [768, 192, 512], P('slab', None, 'grp')
- moments: float32 [2, 512], P(None, 'grp')
Inputs may be any that keep to these rules, and one draw needn't show every extreme that they name: Block b lies in slab b // 12; each of its neighbours lies in the same slab or in one of the two slabs beside it, the last slab being beside the first.
All inputs are finite; a program needn't handle non-finite values.
Results may differ from a plain program's by a relative error of at most 0.0003.
Values may be sent and summed in bfloat16 or wider, within the bound.
A program may use at most 192 MiB of HBM per device.

v0:
```python
import math
import jax
import jax.numpy as jnp
from jax import lax
from jax.sharding import PartitionSpec as P


def with_halo(value, sides, width):
    for axis, dim in sides:
        size, length = (lax.axis_size(axis), value.shape[dim])
        up = [(i, (i + 1) % size) for i in range(size)]
        down = [(j, i) for i, j in up]
        last = lax.slice_in_dim(value, length - width, length, axis=dim)
        leading = lax.slice_in_dim(value, 0, width, axis=dim)
        before = lax.ppermute(last, axis, up)
        after = lax.ppermute(leading, axis, down)
        value = jnp.concatenate([before, value, after], axis=dim)
    return value


def apply_rows(tile_rows, padded, locals_rows):
    width = padded.shape[1]
    squares = tile_rows.reshape(tile_rows.shape[:2] + (width, width))
    near = jnp.take(padded, locals_rows.reshape(-1), axis=0)
    near = near.reshape(locals_rows.shape + padded.shape[1:])
    return jnp.einsum("bkrc,bkcp->brp", squares, near, preferred_element_type=jnp.float32)


def shards(tiles, neighbours, t_cur, t_prev, probes):
    blocks_slab = t_cur.shape[0]
    slab_count = lax.axis_size("slab")
    my_slab = lax.axis_index("slab")
    slab_near = neighbours // blocks_slab
    local_ids = (slab_near - my_slab + 1) % slab_count * blocks_slab + neighbours % blocks_slab
    rows_dev = tiles.shape[0]
    mine = lax.dynamic_slice_in_dim(local_ids, lax.axis_index("grp") * rows_dev, rows_dev, 0)
    whole = lax.all_gather(t_cur, "grp", axis=2, tiled=True)
    padded = with_halo(whole, (("slab", 0),), blocks_slab)
    rows_image = apply_rows(tiles, padded, mine)
    image = lax.all_to_all(rows_image, "grp", split_axis=2, concat_axis=0, tiled=True)
    t_next = 2.0 * image - t_prev
    first = jnp.sum(probes * t_next, axis=(0, 1))
    second = jnp.sum(t_cur.astype(jnp.float32) * t_next, axis=(0, 1))
    first, second = lax.psum((first, second), "slab")
    factor = 1.0 / math.sqrt(slab_count * blocks_slab * t_cur.shape[1])
    moments = jnp.stack([first, second]) * factor
    return (t_next, moments)


def solution(mesh):
    placed = (
        P(("slab", "grp"), None, None),
        P("slab", None),
        P("slab", None, "grp"),
        P("slab", None, "grp"),
        P("slab", None, "grp"),
    )
    return jax.shard_map(
        shards,
        mesh=mesh,
        in_specs=placed,
        out_specs=(P("slab", None, "grp"), P(None, "grp")),
        check_vma=False,
    )
```

profile of v0, /device:TPU:0, one launch (start us, length us, event | category | flops | bytes accessed | tf_op | source)
XLA Modules:
  0.0 328.1 jit_solution(8495705729886352172)
XLA Ops:
  7.2 0.0 all-gather.2.cloned.1.call-start
  7.2 0.7 all-gather.2.cloned.1.call-update
  7.9 34.1 %all-gather.2.cloned.1.call-done = bf16[12,192,512]{2,1,0:T(8,128)(2,1)} async-done(((bf16[12,192,128]{2,1,0:T(8,128)(2,1)}), bf16[12,192,512]{2,1,0:T(8,128)(2,1)}) %all-gather.2.cloned.1.call-update) | async-done | bytes 2359312 | tf_op jit(solution)/shard_map/all_gather | solution.py:37
  42.0 1.6 collective-permute-start
  43.6 4.7 %collective-permute-start.1 = (bf16[12,192,512]{2,1,0:T(8,128)(2,1)}, bf16[12,192,512]{2,1,0:T(8,128)(2,1)}, u32[]{:S(2)}, u32[]{:S(2)}) collective-permute-start(bf16[12,192,512]{2,1,0:T(8,128)(2,1)} %all-gather.2.cloned.1.call-done), channel_id=1, source_target_pairs={{4,0},{8,4},{12,8},{16,12},{20,16},{24,20},{28,24},{32,28},{36,32}... | collective-permute-start | bytes 7077896 | tf_op jit(solution)/shard_map/ppermute | solution.py:16
  48.3 0.7 broadcast_compare_fusion
  49.0 0.7 fusion.16
  49.7 0.1 reshape.51
  49.8 0.0 copy-start
  49.8 12.2 %reshape.52 = bf16[3,27,192,192]{3,2,1,0:T(8,128)(2,1)} reshape(bf16[3,27,36864]{2,1,0:T(8,128)(2,1)} %param.5) | data formatting | bytes 11943936 | tf_op jit(solution)/shard_map/reshape | solution.py:23
  62.0 37.9 %collective-permute-done = bf16[12,192,512]{2,1,0:T(8,128)(2,1)} collective-permute-done((bf16[12,192,512]{2,1,0:T(8,128)(2,1)}, bf16[12,192,512]{2,1,0:T(8,128)(2,1)}, u32[]{:S(2)}, u32[]{:S(2)}) %collective-permute-start) | collective-permute-done | bytes 2359328 | tf_op jit(solution)/shard_map/ppermute | solution.py:15
  100.0 0.0 collective-permute-done.1
  100.0 0.0 copy-done
  100.0 5.9 %pad_maximum_fusion = bf16[36,192,512]{2,1,0:T(8,128)(2,1)} fusion(bf16[12,192,512]{2,1,0:T(8,128)(2,1)} %collective-permute-done.1, bf16[12,192,512]{2,1,0:T(8,128)(2,1)S(1)} %copy-done, bf16[12,192,512]{2,1,0:T(8,128)(2,1)} %collective-permute-done), kind=kLoop, calls=%fused_computation.5 | loop fusion | flops 7077888 | bytes 14155776 | tf_op jit(solution)/shard_map/concatenate | solution.py:17
  105.8 11.3 %gather_fusion = bf16[81,192,512]{2,1,0:T(8,128)(2,1)} fusion(bf16[36,192,512]{2,1,0:T(8,128)(2,1)} %pad_maximum_fusion, s32[1024]{0:T(1024)S(1)} %pad_clamp_fusion), kind=kCustom, calls=%fused_computation | custom fusion | bytes 31850820 | tf_op jit(solution)/shard_map/jit(_take)/gather | solution.py:24
  117.2 10.4 %fusion.4 = f32[3,192,512]{2,1,0:T(8,128)S(1)} fusion(bf16[3,27,192,192]{3,2,1,0:T(8,128)(2,1)} %reshape.52, bf16[3,27,192,512]{3,2,1,0:T(8,128)(2,1)} %bitcast.17, pred[3,27]{1,0:T(4,128)(4,1)S(1)} %get-tuple-element.7), kind=kOutput, calls=%fused_computation.6 | convolution fusion | flops 3065610240 | bytes 23076944 | tf_op jit(solution)/shard_map/bkrc,bkcp->brp/dot_general | solution.py:26
  127.6 0.9 copy.8
  128.5 29.9 %all_to_all.4 = f32[3,192,512]{1,0,2:T(4,128)S(1)} all-to-all(f32[3,192,512]{1,0,2:T(4,128)S(1)} %copy.8), channel_id=1, replica_groups=mesh['slab'=64,'grp'=4] {'grp'}, dimensions={2} | all-to-all | bytes 2359296 | tf_op jit(solution)/shard_map/all_to_all | solution.py:40
  158.4 0.5 broadcast_multiply_fusion
  158.8 0.7 copy.9
  159.5 3.1 multiply_reduce_fusion.1
  162.6 158.1 %all-reduce = (f32[1,128]{1,0:T(1,128)S(1)}, f32[1,128]{1,0:T(1,128)S(1)}) all-reduce(f32[1,128]{1,0:T(1,128)S(1)} %bitcast.20, f32[1,128]{1,0:T(1,128)S(1)} %bitcast.19), channel_id=1, replica_groups=mesh['slab'=64,'grp'=4] {'slab'}, use_global_device_ids=true, to_apply=%region_3.4 | all-reduce | flops 256 | bytes 2048 | tf_op jit(solution)/shard_map/psum | solution.py:44
  320.7 0.6 maximum_multiply_fusion
  (3 shorter events, 0.0 us)
Async XLA Ops:
  7.2 34.8 %all-gather.2.cloned.1.call-start = ((), (), s32[]{:S(2)}) async-start(), calls=%async_computation.1 | async-start | bytes 2949120 | tf_op jit(solution)/shard_map/all_gather | solution.py:37
  42.0 57.9 %collective-permute-start = (bf16[12,192,512]{2,1,0:T(8,128)(2,1)}, bf16[12,192,512]{2,1,0:T(8,128)(2,1)}, u32[]{:S(2)}, u32[]{:S(2)}) collective-permute-start(bf16[12,192,512]{2,1,0:T(8,128)(2,1)} %all-gather.2.cloned.1.call-done), channel_id=1, source_target_pairs={{0,4},{4,8},{8,12},{12,16},{16,20},{20,24},{24,28},{28,32},{32,36}... | collective-permute-start | bytes 7077896 | tf_op jit(solution)/shard_map/ppermute | solution.py:15
  43.6 56.4 %collective-permute-start.1 = (bf16[12,192,512]{2,1,0:T(8,128)(2,1)}, bf16[12,192,512]{2,1,0:T(8,128)(2,1)}, u32[]{:S(2)}, u32[]{:S(2)}) collective-permute-start(bf16[12,192,512]{2,1,0:T(8,128)(2,1)} %all-gather.2.cloned.1.call-done), channel_id=1, source_target_pairs={{4,0},{8,4},{12,8},{16,12},{20,16},{24,20},{28,24},{32,28},{36,32}... | collective-permute-start | bytes 7077896 | tf_op jit(solution)/shard_map/ppermute | solution.py:16
  49.8 50.2 %copy-start = (bf16[12,192,512]{2,1,0:T(8,128)(2,1)S(1)}, bf16[12,192,512]{2,1,0:T(8,128)(2,1)}, u32[]{:S(2)}) copy-start(bf16[12,192,512]{2,1,0:T(8,128)(2,1)} %all-gather.2.cloned.1.call-done) | copy-start | bytes 7077892
Sparse Core Ops, SparseCore 0:
  9.8 32.1 all-gather.1
where the time goes:
time: 329 us; the launch traced here: 328 us
  blocking collectives  188 us (57%)
  waiting for transfers between devices  72.7 us (22%)
  local copies, waits for them, and re-layouts  25.3 us (8%)
  between operations  14.1 us (4%)
  other arithmetic  11.5 us (3%)
  matrix products  10.4 us (3%)
  starting transfers between devices  6.28 us (2%)
    psum x1, blocking collectives, shards(): first, second = lax.psum((first, second), 'slab')  158 us
    ppermute x1, waiting for transfers between devices, with_halo(): before = lax.ppermute(last, axis, up)  37.9 us
    all_gather x1, waiting for transfers between devices, shards(): whole = lax.all_gather(t_cur, 'grp', axis=2, tiled=True)  34.1 us
    all_to_all x1, blocking collectives, shards(): lax.all_to_all(rows_image, 'grp', split_axis=2, concat_axis=0, tiled=True)  29.9 us
    reshape x1, local copies, waits for them, and re-layouts, apply_rows(): squares = tile_rows.reshape(tile_rows.shape[:2] + (width, width))  12.2 us
    gather x1, local copies, waits for them, and re-layouts, apply_rows(): near = jnp.take(padded, locals_rows.reshape(-1), axis=0)  11.3 us
    dot_general x1, matrix products, apply_rows(): jnp.einsum('bkrc,bkcp->brp', squares, near, preferred_element_type=jnp.fl...  10.4 us
  transfers between devices with their start and end apart: 3, of which 2 were waited for; matrix products, arithmetic and copies ran while one was open for 4% of the time, Pallas kernels for 0%

commit v1 on v0

--- a/solution.py
+++ b/solution.py
@@ -34,7 +34,10 @@
     local_ids = (slab_near - my_slab + 1) % slab_count * blocks_slab + neighbours % blocks_slab
     rows_dev = tiles.shape[0]
     mine = lax.dynamic_slice_in_dim(local_ids, lax.axis_index("grp") * rows_dev, rows_dev, 0)
-    whole = lax.all_gather(t_cur, "grp", axis=2, tiled=True)
+    devices = lax.axis_size("grp")
+    blocks = jnp.stack([t_cur for _ in range(devices)])
+    blocks = lax.all_to_all(blocks, "grp", split_axis=0, concat_axis=0)
+    whole = jnp.concatenate(blocks, axis=2)
     padded = with_halo(whole, (("slab", 0),), blocks_slab)
     rows_image = apply_rows(tiles, padded, mine)
     image = lax.all_to_all(rows_image, "grp", split_axis=2, concat_axis=0, tiled=True)

time: 329 us -> 316 us (0.960)
  waiting for transfers between devices: 72.7 us -> 38.7 us
  blocking collectives: 188 us -> 221 us
  between operations: 14.1 us -> 0.69 us
    all_gather x1 -> x0, waiting for transfers between devices: 34.1 us -> none  [shards(): whole = lax.all_gather(t_cur, 'grp', axis=2, tiled=True)]
    all_to_all x0 -> x1, blocking collectives: none -> 32.5 us  [shards(): blocks = lax.all_to_all(blocks, 'grp', split_axis=0, concat_axis=0)]
  transfers between devices with their start and end apart: 3 -> 2, of which waited for: 2 -> 1; matrix products, arithmetic and copies ran while one was open for 4% -> 4% of each run, Pallas kernels for 0% -> 0%
where the time goes in v1:
time: 316 us
  blocking collectives  221 us (70%)
  waiting for transfers between devices  38.7 us (12%)
  local copies, waits for them, and re-layouts  27.1 us (9%)
  matrix products  10.4 us (3%)
  other arithmetic  10 us (3%)
  starting transfers between devices  8.38 us (3%)
    psum x1, blocking collectives, shards(): first, second = lax.psum((first, second), 'slab')  158 us
    ppermute x1, waiting for transfers between devices, with_halo(): before = lax.ppermute(last, axis, up)  38.6 us
    all_to_all x1, blocking collectives, shards(): blocks = lax.all_to_all(blocks, 'grp', split_axis=0, concat_axis=0)  32.5 us
    all_to_all x1, blocking collectives, shards(): lax.all_to_all(rows_image, 'grp', split_axis=2, concat_axis=0, tiled=True)  29.7 us
    reshape x1, local copies, waits for them, and re-layouts, apply_rows(): squares = tile_rows.reshape(tile_rows.shape[:2] + (width, width))  12.1 us
    gather x1, local copies, waits for them, and re-layouts, apply_rows(): near = jnp.take(padded, locals_rows.reshape(-1), axis=0)  11.3 us
    dot_general x1, matrix products, apply_rows(): jnp.einsum('bkrc,bkcp->brp', squares, near, preferred_element_type=jnp.fl...  10.4 us
    ppermute x1, starting transfers between devices, with_halo(): after = lax.ppermute(leading, axis, down)  6.51 us
  transfers between devices with their start and end apart: 2, of which 1 were waited for; matrix products, arithmetic and copies ran while one was open for 4% of the time, Pallas kernels for 0%

profile of v1, /device:TPU:0, one launch (start us, length us, event | category | flops | bytes accessed | tf_op | source)
XLA Modules:
  0.0 315.7 jit_solution(9845473239247121375)
XLA Ops:
  0.6 1.6 stack.16
  2.3 32.5 %all_to_all.14 = bf16[4,12,192,128]{3,2,1,0:T(8,128)(2,1)S(1)} all-to-all(bf16[4,12,192,128]{3,2,1,0:T(8,128)(2,1)S(1)} %stack.16), channel_id=1, replica_groups=mesh['slab'=64,'grp'=4] {'grp'}, dimensions={0} | all-to-all | bytes 4718592 | tf_op jit(solution)/shard_map/all_to_all | solution.py:39
  34.7 0.0 copy-start
  34.7 0.3 copy_bitcast_fusion
  35.1 1.9 collective-permute-start
  36.9 6.5 %collective-permute-start.1 = (bf16[12,192,512]{2,1,0:T(8,128)(2,1)S(1)}, bf16[12,192,512]{2,1,0:T(8,128)(2,1)}, u32[]{:S(2)}, u32[]{:S(2)}) collective-permute-start(bf16[12,192,512]{2,1,0:T(8,128)(2,1)S(1)} %copy_bitcast_fusion), channel_id=1, source_target_pairs={{4,0},{8,4},{12,8},{16,12},{20,16},{24,20},{28,24},{32,28},{36,32}... | collective-permute-start | bytes 7077896 | tf_op jit(solution)/shard_map/ppermute | solution.py:16
  43.4 0.0 copy-done
  43.5 0.1 reshape.61
  43.6 12.1 %reshape.62 = bf16[3,27,192,192]{3,2,1,0:T(8,128)(2,1)} reshape(bf16[3,27,36864]{2,1,0:T(8,128)(2,1)} %param.5) | data formatting | bytes 11943936 | tf_op jit(solution)/shard_map/reshape | solution.py:23
  55.7 38.6 %collective-permute-done = bf16[12,192,512]{2,1,0:T(8,128)(2,1)} collective-permute-done((bf16[12,192,512]{2,1,0:T(8,128)(2,1)S(1)}, bf16[12,192,512]{2,1,0:T(8,128)(2,1)}, u32[]{:S(2)}, u32[]{:S(2)}) %collective-permute-start) | collective-permute-done | bytes 2359328 | tf_op jit(solution)/shard_map/ppermute | solution.py:15
  94.3 0.0 collective-permute-done.1
  94.3 5.8 %pad_maximum_fusion = bf16[36,192,512]{2,1,0:T(8,128)(2,1)} fusion(bf16[12,192,512]{2,1,0:T(8,128)(2,1)} %collective-permute-done.1, bf16[12,192,512]{2,1,0:T(8,128)(2,1)S(1)} %copy_bitcast_fusion, bf16[12,192,512]{2,1,0:T(8,128)(2,1)} %collective-permute-done), kind=kLoop, calls=%fused_computation.5 | loop fusion | flops 7077888 | bytes 14155776 | tf_op jit(solution)/shard_map/concatenate | solution.py:17
  100.2 11.3 %gather_fusion = bf16[81,192,512]{2,1,0:T(8,128)(2,1)} fusion(bf16[36,192,512]{2,1,0:T(8,128)(2,1)} %pad_maximum_fusion, s32[1024]{0:T(1024)S(1)} %pad_clamp_fusion), kind=kCustom, calls=%fused_computation | custom fusion | bytes 31850820 | tf_op jit(solution)/shard_map/jit(_take)/gather | solution.py:24
  111.5 10.4 %fusion.4 = f32[3,192,512]{2,1,0:T(8,128)S(1)} fusion(bf16[3,27,192,192]{3,2,1,0:T(8,128)(2,1)} %reshape.62, bf16[3,27,192,512]{3,2,1,0:T(8,128)(2,1)} %bitcast.23, pred[3,27]{1,0:T(4,128)(4,1)S(1)} %get-tuple-element.7), kind=kOutput, calls=%fused_computation.7 | convolution fusion | flops 3065610240 | bytes 23076944 | tf_op jit(solution)/shard_map/bkrc,bkcp->brp/dot_general | solution.py:26
  121.9 0.9 copy.10
  122.9 29.7 %all_to_all.15 = f32[3,192,512]{1,0,2:T(4,128)S(1)} all-to-all(f32[3,192,512]{1,0,2:T(4,128)S(1)} %copy.10), channel_id=1, replica_groups=mesh['slab'=64,'grp'=4] {'grp'}, dimensions={2} | all-to-all | bytes 2359296 | tf_op jit(solution)/shard_map/all_to_all | solution.py:43
  152.6 0.5 broadcast_multiply_fusion
  153.0 0.7 copy.11
  153.7 3.1 multiply_reduce_fusion.1
  156.8 158.3 %all-reduce = (f32[1,128]{1,0:T(1,128)S(1)}, f32[1,128]{1,0:T(1,128)S(1)}) all-reduce(f32[1,128]{1,0:T(1,128)S(1)} %bitcast.26, f32[1,128]{1,0:T(1,128)S(1)} %bitcast.25), channel_id=1, replica_groups=mesh['slab'=64,'grp'=4] {'slab'}, use_global_device_ids=true, to_apply=%region_3.4 | all-reduce | flops 256 | bytes 2048 | tf_op jit(solution)/shard_map/psum | solution.py:47
  315.2 0.6 maximum_multiply_fusion
  (5 shorter events, 0.1 us)
Async XLA Ops:
  34.7 8.7 %copy-start = (s32[12,27]{1,0:T(8,128)S(1)}, s32[12,27]{1,0:T(8,128)}, u32[]{:S(2)}) copy-start(s32[12,27]{1,0:T(8,128)} %param.6) | copy-start | bytes 3892
  35.1 59.3 %collective-permute-start = (bf16[12,192,512]{2,1,0:T(8,128)(2,1)S(1)}, bf16[12,192,512]{2,1,0:T(8,128)(2,1)}, u32[]{:S(2)}, u32[]{:S(2)}) collective-permute-start(bf16[12,192,512]{2,1,0:T(8,128)(2,1)S(1)} %copy_bitcast_fusion), channel_id=1, source_target_pairs={{0,4},{4,8},{8,12},{12,16},{16,20},{20,24},{24,28},{28,32},{32,36}... | collective-permute-start | bytes 7077896 | tf_op jit(solution)/shard_map/ppermute | solution.py:15
  36.9 57.4 %collective-permute-start.1 = (bf16[12,192,512]{2,1,0:T(8,128)(2,1)S(1)}, bf16[12,192,512]{2,1,0:T(8,128)(2,1)}, u32[]{:S(2)}, u32[]{:S(2)}) collective-permute-start(bf16[12,192,512]{2,1,0:T(8,128)(2,1)S(1)} %copy_bitcast_fusion), channel_id=1, source_target_pairs={{4,0},{8,4},{12,8},{16,12},{20,16},{24,20},{28,24},{32,28},{36,32}... | collective-permute-start | bytes 7077896 | tf_op jit(solution)/shard_map/ppermute | solution.py:16
